TPU v7x, 32 devices: a whole 2x2x4 slice. The times are simulated.
32 devices in a mesh: row: 8 (over y, x, core), rep: 4 (over z).
Axes of the slice: x: 2, y: 2, z: 4, core: 2. Of those that a mesh axis runs over, the one named last changes fastest.
Arguments:
- features: bfloat16 [8192, 256], P('row'), may hold values from -6 to 6
- weight_self: bfloat16 [256, 256], replicated, may hold values from -0.375 to 0.375
- weight_neigh: bfloat16 [256, 256], replicated, may hold values from -0.375 to 0.375
- degrees: int32 [8192], P('row'), may hold values from 1 to 47
- tile_values: bfloat16 [8, 8, 48, 128, 128], P('row', 'rep'), may hold values from 0 to 1
- tile_blocks: int32 [8, 8, 48, 2], P('row', 'rep'), may hold values from 0 to 7
- tile_count: int32 [8, 8], P('row', 'rep'), may hold values from 1 to 48, as said below
- cotangent: bfloat16 [8192, 256], P(('row', 'rep')), may hold values from -6 to 6
Outputs:
- output: bfloat16 [8192, 256], P(('row', 'rep'))
- grad_self: float32 [256, 256], replicated
- grad_neigh: float32 [256, 256], replicated
- grad_features: bfloat16 [8192, 256], P(('row', 'rep'))
Inputs may be any that keep to these rules, and one draw needn't show every extreme that they name: `tile_count`: for some row index and section all 48 slots are live in every draw.
All inputs are finite; a program needn't handle non-finite values.
Results may differ from a plain program's by a relative error of at most 0.024.
Values may be sent and summed in bfloat16 or wider, within the bound.
A program may use at most 64 MiB of HBM per device.

v0:
```python
import jax
import jax.numpy as jnp
from jax import lax
from jax.sharding import PartitionSpec as P


def from_root(value, axis, source):
    kept = jnp.where(lax.axis_index(axis) == source, value, 0).astype(value.dtype)
    return lax.psum(kept, axis)


def hot_tables(blocks, count, nblk, slots):
    live = (jnp.arange(slots) < count).astype(jnp.float32)
    dest_hot = (blocks[:, 0][:, None] == jnp.arange(nblk)[None, :]).astype(jnp.float32) * live[
        :, None
    ]
    src_hot = (blocks[:, 1][:, None] == jnp.arange(nblk)[None, :]).astype(jnp.float32)
    return (dest_hot, src_hot)


def body(
    features, weight_self, weight_neigh, degrees, tile_values, tile_blocks, tile_count, cotangent
):
    rows, width = features.shape
    tile = tile_values.shape[3]
    slots = tile_values.shape[2]
    sections_here = tile_values.shape[1]
    nblk = rows // tile
    nrep = lax.axis_size("rep")
    share = rows // nrep
    rep_pos = lax.axis_index("rep")
    row_pos = lax.axis_index("row")
    partial_value = jnp.zeros((nblk, tile, width), jnp.float32)
    for section in range(sections_here):
        source = from_root(features, "row", rep_pos * sections_here + section)
        source_blocks = source.reshape(nblk, tile, width)
        dest_hot, src_hot = hot_tables(tile_blocks[0, section], tile_count[0, section], nblk, slots)
        picked = jnp.einsum(
            "tc,cif->tif",
            src_hot.astype(jnp.bfloat16),
            source_blocks,
            preferred_element_type=jnp.bfloat16,
        )
        prod = jnp.einsum(
            "tij,tjf->tif", tile_values[0, section], picked, preferred_element_type=jnp.float32
        )
        partial_value = partial_value + jnp.einsum("tb,tif->bif", dest_hot, prod)
    partial_value = partial_value.reshape(rows, width)
    degree_all = degrees.astype(jnp.float32)[:, None]
    degree_mine = lax.dynamic_slice_in_dim(degree_all, rep_pos * share, share, 0)
    feat_mine = lax.dynamic_slice_in_dim(features, rep_pos * share, share, 0)
    agg_part = lax.psum_scatter(partial_value, "rep", scatter_dimension=0, tiled=True)
    agg_mine = (agg_part / degree_mine).astype(jnp.bfloat16)
    pre = jnp.dot(feat_mine, weight_self, preferred_element_type=jnp.float32) + jnp.dot(
        agg_mine, weight_neigh, preferred_element_type=jnp.float32
    )
    sig = jax.nn.sigmoid(pre)
    gpre_mine = (cotangent.astype(jnp.float32) * sig * (1.0 + pre * (1.0 - sig))).astype(
        jnp.bfloat16
    )
    dagg_mine = (
        jnp.dot(gpre_mine, weight_neigh.T, preferred_element_type=jnp.float32) / degree_mine
    ).astype(jnp.bfloat16)
    dagg_all = lax.all_gather(dagg_mine, "rep", axis=0, tiled=True)
    output = jax.nn.silu(pre).astype(jnp.bfloat16)
    grad_self_part = jnp.dot(feat_mine.T, gpre_mine, preferred_element_type=jnp.float32)
    grad_neigh_part = jnp.dot(agg_mine.T, gpre_mine, preferred_element_type=jnp.float32)
    grad_self, grad_neigh = lax.psum((grad_self_part, grad_neigh_part), ("row", "rep"))
    dagg_blocks = dagg_all.reshape(nblk, tile, width)
    terms = []
    for section in range(sections_here):
        dest_hot, src_hot = hot_tables(tile_blocks[0, section], tile_count[0, section], nblk, slots)
        picked = jnp.einsum(
            "tb,bif->tif",
            dest_hot.astype(jnp.bfloat16),
            dagg_blocks,
            preferred_element_type=jnp.bfloat16,
        )
        contrib = jnp.einsum(
            "tij,tif->tjf", tile_values[0, section], picked, preferred_element_type=jnp.float32
        )
        terms.append(jnp.einsum("tc,tjf->cjf", src_hot, contrib).reshape(rows, width))
    stacked = jnp.stack(terms, 0)
    summed = lax.psum(stacked, "row")
    owned = lax.dynamic_index_in_dim(summed, row_pos % sections_here, 0, keepdims=False).astype(
        jnp.bfloat16
    )
    everyone = from_root(owned, "rep", row_pos // sections_here)
    back_mine = lax.dynamic_slice_in_dim(everyone, rep_pos * share, share, 0)
    grad_features = (
        jnp.dot(gpre_mine, weight_self.T, preferred_element_type=jnp.float32)
        + back_mine.astype(jnp.float32)
    ).astype(jnp.bfloat16)
    return (output, grad_self, grad_neigh, grad_features)


def solution(mesh):
    in_specs = (
        P("row", None),
        P(),
        P(),
        P("row"),
        P("row", "rep", None, None, None),
        P("row", "rep", None, None),
        P("row", "rep"),
        P(("row", "rep"), None),
    )
    out_specs = (P(("row", "rep"), None), P(), P(), P(("row", "rep"), None))
    return jax.shard_map(body, mesh=mesh, in_specs=in_specs, out_specs=out_specs, check_vma=False)
```

profile of v0, /device:TPU:0, one launch (start us, length us, event | category | flops | bytes accessed | tf_op | source)
XLA Modules:
  0.0 399.4 jit_solution(14081113110862203722)
XLA Ops:
  7.2 2.3 broadcast_select_fusion.1
  13.0 57.8 %all-reduce.11.cloned.1.call-done = (bf16[8,128,256]{2,1,0:T(8,128)(2,1)}, bf16[8,128,256]{2,1,0:T(8,128)(2,1)}) async-done(((bf16[8,128,256]{2,1,0:T(8,128)(2,1)}, bf16[8,128,256]{2,1,0:T(8,128)(2,1)}), (bf16[8,128,256]{2,1,0:T(8,128)(2,1)}, bf16[8,128,256]{2,1,0:T(8,128)(2,1)})) %all-reduce.11.cloned.1.call-update) | async-done | bytes 1048592 | tf_op jit(solution)/shard_map/psum | solution.py:9
  70.7 2.1 fusion.31
  72.8 3.3 fusion.12
  76.0 3.8 copy.22
  79.9 2.2 fusion.33
  82.1 3.2 fusion.14
  85.3 4.9 %copy.19 = bf16[48,256,128]{1,0,2:T(8,128)(2,1)} copy(bf16[48,256,128]{2,1,0:T(8,128)(2,1)} %fusion.14) | data formatting | bytes 6291456 | tf_op jit(solution)/shard_map/tij,tjf->tif/dot_general | solution.py:44
  95.3 25.4 %reduce-scatter.2.cloned.1.call-done = f32[256,256]{1,0:T(8,128)} async-done(((f32[1024,256]{1,0:T(8,128)}), f32[256,256]{1,0:T(8,128)}) %reduce-scatter.2.cloned.1.call-update) | async-done | bytes 262160 | tf_op jit(solution)/shard_map/reduce_scatter | solution.py:52
  120.7 1.9 multiply_convert_fusion
  122.9 16.2 %all_gather.3 = bf16[1024,256]{1,0:T(8,128)(2,1)S(1)} all-gather(bf16[256,256]{1,0:T(8,128)(2,1)S(1)} %fusion.28), channel_id=1, replica_groups=mesh['row'=8,'rep'=4] {'rep'}, dimensions={0}, use_global_device_ids=true | all-gather | bytes 655360 | tf_op jit(solution)/shard_map/all_gather | solution.py:64
  140.1 2.7 fusion.35
  142.8 3.1 fusion.10
  145.9 3.8 copy.25
  153.0 3.1 fusion.8
  156.1 3.8 copy.27
  161.3 56.4 %all-reduce.12 = bf16[2,1024,256]{2,1,0:T(8,128)(2,1)S(1)} all-reduce(f32[2,1024,256]{2,1,0:T(8,128)S(1)} %pad_maximum_fusion), channel_id=1, replica_groups=mesh['row'=8,'rep'=4] {'row'}, use_global_device_ids=true, to_apply=%region_5.6 | all-reduce | flops 524288 | bytes 3145728 | tf_op jit(solution)/shard_map/psum | solution.py:84
  218.6 1.8 fusion.39
  220.4 2.0 fusion.77
  222.4 32.1 %all-reduce.7.cloned.1.call-done = bf16[1024,256]{1,0:T(8,128)(2,1)} async-done(((bf16[1024,256]{1,0:T(8,128)(2,1)}), bf16[1024,256]{1,0:T(8,128)(2,1)}) %all-reduce.7.cloned.1.call-update) | async-done | bytes 524304 | tf_op jit(solution)/shard_map/psum | solution.py:9
  254.5 1.8 fusion.27
  256.3 133.3 %all-reduce.9.cloned.1.call-done = (f32[256,256]{1,0:T(8,128)}, f32[256,256]{1,0:T(8,128)}) async-done(((f32[256,256]{1,0:T(8,128)}, f32[256,256]{1,0:T(8,128)}), (f32[256,256]{1,0:T(8,128)}, f32[256,256]{1,0:T(8,128)})) %all-reduce.9.cloned.1.call-update) | async-done | bytes 524304 | tf_op jit(solution)/shard_map/psum | solution.py:68
  389.6 1.7 copy.51
  391.2 1.7 copy.52
  (61 shorter events, 15.1 us)
Async XLA Ops:
  7.2 113.6 %copy-start = (bf16[256,256]{1,0:T(8,128)(2,1)S(1)}, bf16[256,256]{1,0:T(8,128)(2,1)}, u32[]{:S(2)}) copy-start(bf16[256,256]{1,0:T(8,128)(2,1)} %param.10) | copy-start | bytes 393220
  7.2 63.5 %all-reduce.11.cloned.1.call-start = ((), (), s32[]{:S(2)}) async-start(), calls=%async_computation.4 | async-start | bytes 2097152 | tf_op jit(solution)/shard_map/psum | solution.py:9
  7.2 65.5 %copy-start.3 = (bf16[1,2,48,128,128]{4,3,2,1,0:T(8,128)(2,1)S(1)}, bf16[1,2,48,128,128]{4,3,2,1,0:T(8,128)(2,1)}, u32[]{:S(2)}) copy-start(bf16[1,2,48,128,128]{4,3,2,1,0:T(8,128)(2,1)} %param.12) | copy-start | bytes 9437188
  9.5 111.2 %reduce-scatter.2.cloned.1.call-start = ((), (), s32[]{:S(2)}) async-start(), calls=%async_computation.1 | async-start | bytes 1310720 | tf_op jit(solution)/shard_map/reduce_scatter | solution.py:52
  11.6 78.7 %copy-start.10 = (bf16[48]{0:T(256)(128)(2,1)}, bf16[48]{0:T(256)(128)(2,1)S(1)}, u32[]{:S(2)}) copy-start(bf16[48]{0:T(256)(128)(2,1)S(1)} %compare_convert_fusion) | copy-start | bytes 292
  12.2 78.5 %copy-start.12 = (bf16[48]{0:T(256)(128)(2,1)}, bf16[48]{0:T(256)(128)(2,1)S(1)}, u32[]{:S(2)}) copy-start(bf16[48]{0:T(256)(128)(2,1)S(1)} %compare_convert_fusion.1) | copy-start | bytes 292
  79.9 2.2 copy-start.4
  90.2 1.9 copy-start.1
  92.1 1.9 copy-start.9
  92.1 2.1 copy-start.8
  92.7 28.1 %copy-start.16 = (bf16[256,256]{1,0:T(8,128)(2,1)S(1)}, bf16[256,256]{1,0:T(8,128)(2,1)}, u32[]{:S(2)}) copy-start(bf16[256,256]{1,0:T(8,128)(2,1)} %param.15) | copy-start | bytes 393220
  94.0 45.1 %copy-start.13 = (bf16[48]{0:T(256)(128)(2,1)S(1)}, bf16[48]{0:T(256)(128)(2,1)}, u32[]{:S(2)}) copy-start(bf16[48]{0:T(256)(128)(2,1)} %copy-done.12) | copy-start | bytes 292
  94.0 160.5 %all-reduce.7.cloned.1.call-start = ((), (), s32[]{:S(2)}) async-start(), calls=%async_computation.2 | async-start | bytes 1048576 | tf_op jit(solution)/shard_map/psum | solution.py:9
  94.2 45.9 %copy-start.14 = (f32[256]{0:T(256)}, f32[256]{0:T(256)S(1)}, u32[]{:S(2)}) copy-start(f32[256]{0:T(256)S(1)} %dynamic-slice.3) | copy-start | bytes 3076
  122.7 17.5 %copy-start.11 = (bf16[48]{0:T(256)(128)(2,1)S(1)}, bf16[48]{0:T(256)(128)(2,1)}, u32[]{:S(2)}) copy-start(bf16[48]{0:T(256)(128)(2,1)} %copy-done.10) | copy-start | bytes 292
  139.1 3.7 copy-start.5
  149.8 2.1 copy-start.2
  149.8 3.2 copy-start.6
  159.9 1.2 copy-start.7
  161.3 59.1 %copy-start.15 = (f32[256]{0:T(256)S(1)}, f32[256]{0:T(256)}, u32[]{:S(2)}) copy-start(f32[256]{0:T(256)} %copy-done.14) | copy-start | bytes 3076
  218.5 171.0 %all-reduce.9.cloned.1.call-start = ((), (), s32[]{:S(2)}) async-start(), calls=%async_computation.3 | async-start | bytes 1048576 | tf_op jit(solution)/shard_map/psum | solution.py:68
Sparse Core Ops, SparseCore 0:
  11.2 59.4 all-reduce.10
  94.1 26.5 reduce-scatter.1
  218.7 35.8 all-reduce.6
  260.4 129.1 all-reduce.8
where the time goes:
time: 400 us; the launch traced here: 399 us
  waiting for transfers between devices  249 us (62%)
  blocking collectives  72.6 us (18%)
  matrix products  31.5 us (8%)
  local copies, waits for them, and re-layouts  28 us (7%)
  between operations  14 us (4%)
  other arithmetic  4.54 us (1%)
    psum x1, waiting for transfers between devices, body(): lax.psum((grad_self_part, grad_neigh_part), ('row', 'rep'))  133 us
    psum x2, waiting for transfers between devices, from_root(): return lax.psum(kept, axis)  89.8 us
    psum x1, blocking collectives, body(): summed = lax.psum(stacked, 'row')  56.4 us
    reduce_scatter x1, waiting for transfers between devices, body(): lax.psum_scatter(partial_value, 'rep', scatter_dimension=0, tiled=True)  25.4 us
    all_gather x1, blocking collectives, body(): dagg_all = lax.all_gather(dagg_mine, 'rep', axis=0, tiled=True)  16.2 us
    dot_general x2, local copies, waits for them, and re-layouts, body(): jnp.einsum('tij,tjf->tif', tile_values[0, section], picked, preferred_ele...  8.77 us
  transfers between devices with their start and end apart: 4, of which 4 were waited for; matrix products, arithmetic and copies ran while one was open for 3% of the time, Pallas kernels for 0%

commit v1 on v0

--- a/solution.py
+++ b/solution.py
@@ -6,7 +6,7 @@
 
 def from_root(value, axis, source):
     kept = jnp.where(lax.axis_index(axis) == source, value, 0).astype(value.dtype)
-    return lax.psum(kept, axis)
+    return jnp.sum(lax.all_gather(kept, axis), axis=0)
 
 
 def hot_tables(blocks, count, nblk, slots):

time: 400 us -> 419 us (1.048)
  other arithmetic: 4.54 us -> 14.2 us
  waiting for transfers between devices: 249 us -> 258 us
    all_gather x0 -> x3, waiting for transfers between devices: none -> 100 us  [from_root(): return jnp.sum(lax.all_gather(kept, axis), axis=0)]
    psum x2 -> x0, waiting for transfers between devices: 89.8 us -> none  [from_root(): return lax.psum(kept, axis)]
    reduce_sum x0 -> x3, other arithmetic: none -> 9.75 us  [from_root(): return jnp.sum(lax.all_gather(kept, axis), axis=0)]
  transfers between devices with their start and end apart: 4 -> 5, of which waited for: 4 -> 5; matrix products, arithmetic and copies ran while one was open for 3% -> 6% of each run, Pallas kernels for 0% -> 0%
where the time goes in v1:
time: 419 us; the launch traced here: 418 us
  waiting for transfers between devices  258 us (62%)
  blocking collectives  72.2 us (17%)
  matrix products  30.6 us (7%)
  local copies, waits for them, and re-layouts  28.1 us (7%)
  other arithmetic  14.2 us (3%)
  between operations  14.1 us (3%)
    psum x1, waiting for transfers between devices, body(): lax.psum((grad_self_part, grad_neigh_part), ('row', 'rep'))  131 us
    all_gather x3, waiting for transfers between devices, from_root(): return jnp.sum(lax.all_gather(kept, axis), axis=0)  100 us
    psum x1, blocking collectives, body(): summed = lax.psum(stacked, 'row')  56 us
    reduce_scatter x1, waiting for transfers between devices, body(): lax.psum_scatter(partial_value, 'rep', scatter_dimension=0, tiled=True)  26.2 us
    all_gather x1, blocking collectives, body(): dagg_all = lax.all_gather(dagg_mine, 'rep', axis=0, tiled=True)  16.2 us
    reduce_sum x3, other arithmetic, from_root(): return jnp.sum(lax.all_gather(kept, axis), axis=0)  9.75 us
    dot_general x2, local copies, waits for them, and re-layouts, body(): jnp.einsum('tij,tjf->tif', tile_values[0, section], picked, preferred_ele...  8.82 us
  transfers between devices with their start and end apart: 5, of which 5 were waited for; matrix products, arithmetic and copies ran while one was open for 6% of the time, Pallas kernels for 0%

profile of v1, /device:TPU:0, one launch (start us, length us, event | category | flops | bytes accessed | tf_op | source)
XLA Modules:
  0.0 417.7 jit_solution(13043994204881829861)
XLA Ops:
  7.2 2.2 broadcast_select_fusion
  13.6 35.6 %all-gather.8.cloned.1.call-done = bf16[8192,256]{1,0:T(8,128)(2,1)} async-done(((bf16[1024,256]{1,0:T(8,128)(2,1)}), bf16[8192,256]{1,0:T(8,128)(2,1)}) %all-gather.8.cloned.1.call-update) | async-done | bytes 4194320 | tf_op jit(solution)/shard_map/all_gather | solution.py:9
  49.2 3.9 reduce_sum.36
  53.1 2.1 fusion.33
  55.1 3.3 fusion.8
  58.5 3.9 copy.30
  62.3 25.4 %all-gather.10.cloned.1.call-done = bf16[8192,256]{1,0:T(8,128)(2,1)} async-done(((bf16[1024,256]{1,0:T(8,128)(2,1)}), bf16[8192,256]{1,0:T(8,128)(2,1)}) %all-gather.10.cloned.1.call-update) | async-done | bytes 4194320 | tf_op jit(solution)/shard_map/all_gather | solution.py:9
  87.7 3.7 reduce_sum.37
  91.4 2.2 fusion.31
  93.7 3.2 fusion.11
  96.9 4.9 %copy.33 = bf16[48,128,256]{2,0,1:T(8,128)(2,1)} copy(bf16[48,128,256]{1,2,0:T(8,128)(2,1)} %fusion.11) | data formatting | bytes 6291456 | tf_op jit(solution)/shard_map/tij,tjf->tif/dot_general | solution.py:44
  106.9 26.2 %reduce-scatter.2.cloned.1.call-done = f32[256,256]{1,0:T(8,128)} async-done(((f32[1024,256]{1,0:T(8,128)}), f32[256,256]{1,0:T(8,128)}) %reduce-scatter.2.cloned.1.call-update) | async-done | bytes 262160 | tf_op jit(solution)/shard_map/reduce_scatter | solution.py:52
  133.0 1.9 multiply_convert_fusion
  135.2 16.2 %all_gather.23 = bf16[1024,256]{1,0:T(8,128)(2,1)S(1)} all-gather(bf16[256,256]{1,0:T(8,128)(2,1)S(1)} %fusion.29), channel_id=1, replica_groups=mesh['row'=8,'rep'=4] {'rep'}, dimensions={0}, use_global_device_ids=true | all-gather | bytes 655360 | tf_op jit(solution)/shard_map/all_gather | solution.py:64
  152.4 2.7 fusion.35
  155.1 3.1 fusion.14
  158.2 3.8 copy.37
  165.3 3.1 fusion.17
  168.4 3.8 copy.41
  173.6 56.0 %all-reduce.5 = bf16[2,1024,256]{2,1,0:T(8,128)(2,1)S(1)} all-reduce(f32[2,1024,256]{2,1,0:T(8,128)S(1)} %pad_maximum_fusion), channel_id=1, replica_groups=mesh['row'=8,'rep'=4] {'row'}, use_global_device_ids=true, to_apply=%region_5.6 | all-reduce | flops 524288 | bytes 3145728 | tf_op jit(solution)/shard_map/psum | solution.py:84
  232.3 2.0 fusion.80
  234.3 39.4 %all-gather.6.cloned.1.call-done = bf16[4,1024,256]{2,1,0:T(8,128)(2,1)} async-done(((bf16[1,1024,256]{2,1,0:T(8,128)(2,1)}), bf16[4,1024,256]{2,1,0:T(8,128)(2,1)}) %all-gather.6.cloned.1.call-update) | async-done | bytes 2097168 | tf_op jit(solution)/shard_map/all_gather | solution.py:9
  273.8 2.2 reduce_sum.38
  276.8 131.0 %all-reduce.4.cloned.1.call-done = (f32[256,256]{1,0:T(8,128)}, f32[256,256]{1,0:T(8,128)}) async-done(((f32[256,256]{1,0:T(8,128)}, f32[256,256]{1,0:T(8,128)}), (f32[256,256]{1,0:T(8,128)}, f32[256,256]{1,0:T(8,128)})) %all-reduce.4.cloned.1.call-update) | async-done | bytes 524304 | tf_op jit(solution)/shard_map/psum | solution.py:68
  (69 shorter events, 21.9 us)
Async XLA Ops:
  7.2 125.9 %copy-start = (bf16[256,256]{1,0:T(8,128)(2,1)S(1)}, bf16[256,256]{1,0:T(8,128)(2,1)}, u32[]{:S(2)}) copy-start(bf16[256,256]{1,0:T(8,128)(2,1)} %param.10) | copy-start | bytes 393220
  7.2 42.0 %all-gather.8.cloned.1.call-start = ((), (), s32[]{:S(2)}) async-start(), calls=%async_computation.3 | async-start | bytes 4718592 | tf_op jit(solution)/shard_map/all_gather | solution.py:9
  9.4 78.3 %all-gather.10.cloned.1.call-start = ((), (), s32[]{:S(2)}) async-start(), calls=%async_computation.4 | async-start | bytes 4718592 | tf_op jit(solution)/shard_map/all_gather | solution.py:9
  10.2 122.8 %reduce-scatter.2.cloned.1.call-start = ((), (), s32[]{:S(2)}) async-start(), calls=%async_computation.1 | async-start | bytes 1310720 | tf_op jit(solution)/shard_map/reduce_scatter | solution.py:52
  12.2 89.6 %copy-start.11 = (bf16[48]{0:T(256)(128)(2,1)}, bf16[48]{0:T(256)(128)(2,1)S(1)}, u32[]{:S(2)}) copy-start(bf16[48]{0:T(256)(128)(2,1)S(1)} %compare_convert_fusion.1) | copy-start | bytes 292
  12.9 89.5 %copy-start.13 = (bf16[48]{0:T(256)(128)(2,1)}, bf16[48]{0:T(256)(128)(2,1)S(1)}, u32[]{:S(2)}) copy-start(bf16[48]{0:T(256)(128)(2,1)S(1)} %compare_convert_fusion) | copy-start | bytes 292
  49.2 5.9 %copy-start.4 = (bf16[1,2,48,128,128]{4,3,2,1,0:T(8,128)(2,1)S(1)}, bf16[1,2,48,128,128]{4,3,2,1,0:T(8,128)(2,1)}, u32[]{:S(2)}) copy-start(bf16[1,2,48,128,128]{4,3,2,1,0:T(8,128)(2,1)} %param.12) | copy-start | bytes 9437188
  91.4 2.2 copy-start.5
  101.8 1.9 copy-start.2
  103.7 2.0 copy-start.10
  103.7 2.1 copy-start.9
  104.2 28.8 %copy-start.17 = (bf16[256,256]{1,0:T(8,128)(2,1)S(1)}, bf16[256,256]{1,0:T(8,128)(2,1)}, u32[]{:S(2)}) copy-start(bf16[256,256]{1,0:T(8,128)(2,1)} %param.15) | copy-start | bytes 393220
  105.6 45.8 %copy-start.12 = (bf16[48]{0:T(256)(128)(2,1)S(1)}, bf16[48]{0:T(256)(128)(2,1)}, u32[]{:S(2)}) copy-start(bf16[48]{0:T(256)(128)(2,1)} %copy-done.11) | copy-start | bytes 292
  105.6 168.2 %all-gather.6.cloned.1.call-start = ((), (), s32[]{:S(2)}) async-start(), calls=%async_computation.2 | async-start | bytes 2621440 | tf_op jit(solution)/shard_map/all_gather | solution.py:9
  105.8 46.6 %copy-start.15 = (f32[256]{0:T(256)}, f32[256]{0:T(256)S(1)}, u32[]{:S(2)}) copy-start(f32[256]{0:T(256)S(1)} %dynamic-slice.3) | copy-start | bytes 3076
  135.0 17.5 %copy-start.14 = (bf16[48]{0:T(256)(128)(2,1)S(1)}, bf16[48]{0:T(256)(128)(2,1)}, u32[]{:S(2)}) copy-start(bf16[48]{0:T(256)(128)(2,1)} %copy-done.13) | copy-start | bytes 292
  151.4 3.7 copy-start.6
  162.1 2.1 copy-start.3
  162.1 3.2 copy-start.7
  172.2 1.2 copy-start.8
  173.6 58.7 %copy-start.16 = (f32[256]{0:T(256)S(1)}, f32[256]{0:T(256)}, u32[]{:S(2)}) copy-start(f32[256]{0:T(256)} %copy-done.15) | copy-start | bytes 3076
  230.4 180.8 %copy-start.1 = (bf16[256,256]{1,0:T(8,128)(2,1)S(1)}, bf16[256,256]{1,0:T(8,128)(2,1)}, u32[]{:S(2)}) copy-start(bf16[256,256]{1,0:T(8,128)(2,1)} %param.10) | copy-start | bytes 393220
  230.5 177.4 %all-reduce.4.cloned.1.call-start = ((), (), s32[]{:S(2)}) async-start(), calls=%async_computation.5 | async-start | bytes 1048576 | tf_op jit(solution)/shard_map/psum | solution.py:68
Sparse Core Ops, SparseCore 0:
  9.9 39.2 all-gather.7
  51.1 36.5 all-gather.9
  105.7 27.2 reduce-scatter.1
  230.6 43.1 all-gather.5
  279.6 128.1 all-reduce.3
